TPU v7x, 256 devices: a whole 4x4x8 slice. The times are simulated.
256 devices in a mesh: dp: 32 (over y, z), mp: 8 (over x, core).
Axes of the slice: x: 4, y: 4, z: 8, core: 2. Of those that a mesh axis runs over, the one named last changes fastest.
Arguments:
- inputs: bfloat16 [12288, 4608], P('dp', 'mp'), may hold values from -80 to 80
- queries: bfloat16 [12288, 4096], P('dp', 'mp'), may hold values from -7.5 to 7.5
- keys: bfloat16 [12288, 2048], P('dp', 'mp'), may hold values from -7.5 to 7.5
- values: bfloat16 [12288, 2048], P('dp', 'mp'), may hold values from -6 to 6
- out_weight: bfloat16 [4096, 4608], P('mp'), may hold values from -0.5 to 0.5
- norm_gain: bfloat16 [4608], P('mp'), may hold values from 0.5 to 1.5
- languages: int32 [32, 1], replicated, may hold values from 0 to 7
- lengths: int32 [32], replicated, may hold values from 193 to 384, as said below
- pattern: int32 [32, 3, 3], P('dp'), may hold values from 0 to 1, as said below
Outputs:
- counts: int32 [8], replicated
- mean: float32 [8, 4608], P(None, 'dp')
- co_moment: float32 [8, 4608, 4608], P(None, 'dp', 'mp')
Inputs may be any that keep to these rules, and one draw needn't show every extreme that they name: Each of the 8 languages is the language of one or more sequences. `lengths`: one or more sequences have all 384 tokens live. `pattern`: for each sequence there is a window w of 1 to 3 blocks such that block (q, k) is 1 exactly when q - w < k <= q.
All inputs are finite; a program needn't handle non-finite values.
Results may differ from a plain program's by a relative error of at most 0.01.
Values may be sent and summed in bfloat16 or wider, within the bound.
No kernel may reach another device: no remote copies, remote signals or barrier semaphores. Data moves between devices by JAX's collectives and lax.ppermute only.
A program may use at most 128 MiB of HBM per device.

v0:
```python
import jax
import jax.numpy as jnp
from jax import lax
from jax.sharding import PartitionSpec as P

D = 4608
H = 32
KVH = 16
HD = 128
LANGS = 8
BLK = 128
query_scale = 1.0 / 12.0
softcap = 50.0
epsilon = 1e-06


def visible(blocks, seq_len):
    spread = jnp.repeat(jnp.repeat(blocks, BLK, 0), BLK, 1)
    position = jnp.arange(seq_len)
    return (spread == 1) & (position[None, :] <= position[:, None])


def attend(queries, keys, values, blocks):
    seq_len = queries.shape[0]
    kv_local = keys.shape[1] // HD
    grouped = queries.reshape(seq_len, kv_local, H // KVH, HD)
    keyed = keys.reshape(seq_len, kv_local, HD)
    valued = values.reshape(seq_len, kv_local, HD)
    scores = (
        jnp.einsum("qkgd,tkd->kgqt", grouped, keyed, preferred_element_type=jnp.float32)
        * query_scale
    )
    capped = softcap * jnp.tanh(scores / softcap)
    allowed = visible(blocks, seq_len)
    expo = jnp.where(allowed, jnp.exp(capped), 0.0)
    weights = (expo / jnp.sum(expo, -1, keepdims=True)).astype(jnp.bfloat16)
    mixed = jnp.einsum("kgqt,tkd->qkgd", weights, valued, preferred_element_type=jnp.float32)
    return mixed.astype(jnp.bfloat16).reshape(seq_len, kv_local * (H // KVH) * HD)


def shards(inputs, queries, keys, values, out_weight, norm_gain, languages, lengths, pattern):
    seq_len = queries.shape[0]
    panel = inputs.shape[1]
    data_count = lax.axis_size("dp")
    row_width = D // data_count
    mixed = attend(queries, keys, values, pattern[0])
    output = (
        lax.psum_scatter(
            lax.dot_general(
                out_weight, mixed, (((0,), (1,)), ((), ())), preferred_element_type=jnp.float32
            ).astype(jnp.bfloat16),
            "mp",
            scatter_dimension=0,
            tiled=True,
        )
        .astype(jnp.float32)
        .T
    )
    hidden = inputs.astype(jnp.float32) + output
    square = lax.psum(jnp.sum(hidden * hidden, 1), "mp")
    normed = (
        hidden * lax.rsqrt(square[:, None] / D + epsilon) * norm_gain.astype(jnp.float32)[None, :]
    ).astype(jnp.bfloat16)
    full_rows = lax.all_gather(normed, "mp", axis=1, tiled=True)
    block_rows = lax.all_to_all(
        full_rows.reshape(seq_len, data_count, row_width),
        "dp",
        split_axis=1,
        concat_axis=0,
        tiled=True,
    ).reshape(data_count * seq_len, row_width)
    language = languages[:, 0]
    alive = (jnp.arange(seq_len)[None, :] < lengths[:, None]).astype(jnp.bfloat16)
    alive_flat = alive.reshape(-1)
    masked_rows = block_rows * alive_flat[:, None]
    onehot = language[:, None] == jnp.arange(LANGS)[None, :]
    token_weights = (onehot.astype(jnp.bfloat16)[:, None, :] * alive[:, :, None]).reshape(-1, LANGS)
    row_sums = lax.dot_general(
        token_weights, block_rows, (((0,), (0,)), ((), ())), preferred_element_type=jnp.float32
    )
    counts = jnp.sum(onehot.astype(jnp.int32) * lengths[:, None], 0)
    start_state = (
        jnp.zeros((LANGS, row_width, panel), jnp.float32),
        jnp.zeros((LANGS, panel), jnp.float32),
    )
    piece = lax.all_gather(normed, "dp", axis=0, tiled=True)
    piece_length = piece.shape[0]
    piece_span = min(piece_length, seq_len)
    turn_count = max(1, piece_length // seq_len)

    def one_sequence(turn, state):
        products, panel_sums = state
        offset = turn * piece_span
        piece_part = lax.dynamic_slice_in_dim(piece, offset, piece_span, 0)
        left_rows = lax.dynamic_slice_in_dim(masked_rows, offset, piece_span, 0)
        live_part = lax.dynamic_slice_in_dim(alive_flat, offset, piece_span, 0)
        which = lax.dynamic_index_in_dim(language, offset // seq_len, 0, False)
        term = lax.dot_general(
            left_rows, piece_part, (((0,), (0,)), ((), ())), preferred_element_type=jnp.float32
        )
        products = lax.dynamic_update_index_in_dim(
            products, lax.dynamic_index_in_dim(products, which, 0, False) + term, which, 0
        )
        panel_add = jnp.dot(live_part, piece_part, preferred_element_type=jnp.float32)
        panel_sums = lax.dynamic_update_index_in_dim(
            panel_sums, lax.dynamic_index_in_dim(panel_sums, which, 0, False) + panel_add, which, 0
        )
        return (products, panel_sums)

    products, panel_sums = lax.fori_loop(0, turn_count, one_sequence, start_state)
    scale = counts.astype(jnp.float32)
    mean = row_sums / scale[:, None]
    co_moment = (
        products - row_sums[:, :, None] * panel_sums[:, None, :] / scale[:, None, None]
    ) / scale[:, None, None]
    return (counts, mean, co_moment)


def solution(mesh):
    in_specs = (
        P("dp", "mp"),
        P("dp", "mp"),
        P("dp", "mp"),
        P("dp", "mp"),
        P("mp", None),
        P("mp"),
        P(),
        P(),
        P("dp", None, None),
    )
    out_specs = (P(), P(None, "dp"), P(None, "dp", "mp"))
    return jax.shard_map(shards, mesh=mesh, in_specs=in_specs, out_specs=out_specs, check_vma=False)
```

profile of v0, /device:TPU:1, one launch (start us, length us, event | category | flops | bytes accessed | tf_op | source)
XLA Modules:
  0.0 477.5 jit_solution(18366444567374238282)
XLA Ops:
  12.2 1.2 convolution_convert_fusion.1
  13.4 4.5 fusion.7
  17.9 3.6 copy.71
  22.8 39.3 %reduce-scatter.4.cloned.1.call-done = bf16[576,384]{1,0:T(8,128)(2,1)} async-done(((bf16[4608,384]{1,0:T(8,128)(2,1)}), bf16[576,384]{1,0:T(8,128)(2,1)}) %reduce-scatter.4.cloned.1.call-update) | async-done | bytes 442384
  62.2 1.3 copy.72
  63.7 15.0 %psum.7 = f32[384]{0:T(512)S(1)} all-reduce(f32[384]{0:T(512)S(1)} %multiply_reduce_fusion), channel_id=1, replica_groups=mesh['dp'=32,'mp'=8] {'mp'}, use_global_device_ids=true, to_apply=%region_4.5 | all-reduce | flops 384 | bytes 3072 | tf_op jit(solution)/shard_map/psum | solution.py:60
  80.6 31.0 %all-gather.3.cloned.1.call-done = bf16[384,4608]{0,1:T(8,128)(2,1)} async-done(((bf16[384,576]{0,1:T(8,128)(2,1)}), bf16[384,4608]{0,1:T(8,128)(2,1)}) %all-gather.3.cloned.1.call-update) | async-done | bytes 3538960 | tf_op jit(solution)/shard_map/all_gather | solution.py:64
  111.6 9.7 %all-to-all-start = ((bf16[384,32,144]{0,2,1:T(8,128)(2,1)}), bf16[384,32,144]{0,2,1:T(8,128)(2,1)S(1)}, u32[]{:S(2)}, u32[]{:S(2)}) async-start(bf16[384,32,144]{0,2,1:T(8,128)(2,1)} %bitcast.68), calls=%async_computation | async-start | bytes 7077888 | tf_op jit(solution)/shard_map/all_to_all | solution.py:65
  122.1 1.3 fusion.12
  123.4 1.4 reshape.147
  124.8 1.5 broadcast_multiply_fusion.1
  126.3 92.5 %all-to-all-done = bf16[384,32,144]{0,2,1:T(8,128)(2,1)S(1)} async-done(((bf16[384,32,144]{0,2,1:T(8,128)(2,1)}), bf16[384,32,144]{0,2,1:T(8,128)(2,1)S(1)}, u32[]{:S(2)}, u32[]{:S(2)}) %all-to-all-start) | async-done | bytes 3538976 | tf_op jit(solution)/shard_map/all_to_all | solution.py:65
  219.8 1.6 broadcast_divide_fusion
  221.4 2.0 broadcast_multiply_fusion
  223.4 70.8 %all-gather.5.cloned.1.call-done = bf16[12288,576]{1,0:T(8,128)(2,1)} async-done(((bf16[384,576]{1,0:T(8,128)(2,1)}), bf16[12288,576]{1,0:T(8,128)(2,1)}) %all-gather.5.cloned.1.call-update) | async-done | bytes 14155792 | tf_op jit(solution)/shard_map/all_gather | solution.py:86
  294.5 174.3 %while.17 = (s32[]{:T(128)}, f32[8,144,576]{2,1,0:T(8,128)S(1)}, f32[8,576]{1,0:T(8,128)S(1)}, s32[32]{0:T(128)S(1)}, bf16[12288,144]{0,1:T(8,128)(2,1)}, /*inde...) while((s32[]{:T(128)}, f32[8,144,576]{2,1,0:T(8,128)S(1)}, ...), condition=%wide.region_6.7_spmd, body=%wide.region_5.6_spmd.sunk | while | flops 64226900 | bytes 2523245 | solution.py:110
  297.1 1.4 fusion.31
  302.5 1.4 fusion.31
  304.0 1.2 convolution_reduce_fusion.2
  308.0 1.4 fusion.31
  309.5 1.2 convolution_reduce_fusion.2
  313.4 1.4 fusion.31
  318.9 1.4 fusion.31
  324.3 1.4 fusion.31
  329.8 1.4 fusion.31
  335.2 1.4 fusion.31
  340.7 1.4 fusion.31
  346.1 1.4 fusion.31
  351.6 1.4 fusion.31
  353.1 1.2 convolution_reduce_fusion.2
  357.0 1.4 fusion.31
  358.5 1.2 convolution_reduce_fusion.2
  362.5 1.4 fusion.31
  364.0 1.2 convolution_reduce_fusion.2
  367.9 1.4 fusion.31
  369.4 1.2 convolution_reduce_fusion.2
  373.4 1.4 fusion.31
  374.9 1.2 convolution_reduce_fusion.2
  378.8 1.4 fusion.31
  380.3 1.2 convolution_reduce_fusion.2
  384.2 1.4 fusion.31
  385.8 1.2 convolution_reduce_fusion.2
  389.7 1.4 fusion.31
  391.2 1.2 convolution_reduce_fusion.2
  395.1 1.4 fusion.31
  396.7 1.2 convolution_reduce_fusion.2
  400.6 1.4 fusion.31
  402.1 1.2 convolution_reduce_fusion.2
  406.0 1.4 fusion.31
  407.6 1.2 convolution_reduce_fusion.2
  411.5 1.4 fusion.31
  413.0 1.2 convolution_reduce_fusion.2
  416.9 1.4 fusion.31
  422.4 1.4 fusion.31
  427.8 1.4 fusion.31
  433.3 1.4 fusion.31
  438.7 1.4 fusion.31
  444.2 1.4 fusion.31
  449.6 1.4 fusion.31
  455.1 1.4 fusion.31
  456.6 1.2 convolution_reduce_fusion.2
  460.5 1.4 fusion.31
  466.0 1.4 fusion.31
  468.8 2.1 subtract_divide_fusion
  (319 shorter events, 57.0 us)
Async XLA Ops:
  7.2 55.0 %reduce-scatter.4.cloned.1.call-start = ((), (), s32[]{:S(2)}) async-start(), calls=%async_computation.4 | async-start | bytes 3981312
  21.5 1.0 copy-start.2
  21.5 1.3 copy-start.4
  21.6 90.1 %all-gather.3.cloned.1.call-start = ((), (), s32[]{:S(2)}) async-start(), calls=%async_computation.2 | async-start | bytes 3981312 | tf_op jit(solution)/shard_map/all_gather | solution.py:64
  78.9 1.0 copy-start
  79.9 214.4 %all-gather.5.cloned.1.call-start = ((), (), s32[]{:S(2)}) async-start(), calls=%async_computation.3 | async-start | bytes 16220160 | tf_op jit(solution)/shard_map/all_gather | solution.py:86
  111.6 9.7 %copy-start.5 = (s32[32]{0:T(128)S(1)}, s32[32]{0:T(128)}, u32[]{:S(2)}) copy-start(s32[32]{0:T(128)} %param.18) | copy-start | bytes 388
  111.6 9.7 %copy-start.6 = (s32[32,1]{0,1:T(1,128)S(1)}, s32[32,1]{0,1:T(1,128)}, u32[]{:S(2)}) copy-start(s32[32,1]{0,1:T(1,128)} %param.17) | copy-start | bytes 388
  111.6 107.2 %all-to-all-start = ((bf16[384,32,144]{0,2,1:T(8,128)(2,1)}), bf16[384,32,144]{0,2,1:T(8,128)(2,1)S(1)}, u32[]{:S(2)}, u32[]{:S(2)}) async-start(bf16[384,32,144]{0,2,1:T(8,128)(2,1)} %bitcast.68), calls=%async_computation | async-start | bytes 7077888 | tf_op jit(solution)/shard_map/all_to_all | solution.py:65
  121.5 0.5 copy-start.8
  218.9 0.9 copy-start.1
  219.4 2.0 copy-start.3
  223.4 71.0 %copy-start.7 = (s32[32,1]{0,1:T(1,128)S(1)}, s32[32,1]{0,1:T(1,128)}, u32[]{:S(2)}) copy-start(s32[32,1]{0,1:T(1,128)} %param.17) | copy-start | bytes 388
Sparse Core Ops, SparseCore 0:
  21.7 40.4 reduce-scatter.3
  80.0 31.5 all-gather.2
  114.8 179.3 all-gather.4
where the time goes:
time: 481 us; the launch traced here: 477 us
  waiting for transfers between devices  234 us (49%)
  matrix products  91 us (19%)
  loops' own time  65.3 us (14%)
  local copies, waits for them, and re-layouts  39.5 us (8%)
  blocking collectives  15 us (3%)
  between operations  13.9 us (3%)
  starting transfers between devices  9.82 us (2%)
  other arithmetic  8.46 us (2%)
    all_to_all x1, waiting for transfers between devices, shards(): lax.all_to_all(full_rows.reshape(seq_len, data_count, row_width), 'dp', s...  92.5 us
    all_gather x1, waiting for transfers between devices, shards(): piece = lax.all_gather(normed, 'dp', axis=0, tiled=True)  70.8 us
    another operation x1, loops' own time, shards(): lax.fori_loop(0, turn_count, one_sequence, start_state)  65.3 us
    dot_general x32, matrix products, one_sequence(): lax.dot_general(left_rows, piece_part, (((0,), (0,)), ((), ())), preferre...  44.1 us
    unnamed x4, waiting for transfers between devices  40 us
    dot_general x32, matrix products, one_sequence(): jnp.dot(live_part, piece_part, preferred_element_type=jnp.float32)  38.8 us
    all_gather x1, waiting for transfers between devices, shards(): full_rows = lax.all_gather(normed, 'mp', axis=1, tiled=True)  31 us
    dynamic_slice x32, local copies, waits for them, and re-layouts, one_sequence(): which = lax.dynamic_index_in_dim(language, offset // seq_len, 0, False)  18.8 us
  transfers between devices with their start and end apart: 4, of which 4 were waited for; matrix products, arithmetic and copies ran while one was open for 2% of the time, Pallas kernels for 0%

commit v1 on v0

--- a/solution.py
+++ b/solution.py
@@ -1,3 +1,4 @@
+import functools
 import jax
 import jax.numpy as jnp
 from jax import lax
@@ -12,6 +13,18 @@
 query_scale = 1.0 / 12.0
 softcap = 50.0
 epsilon = 1e-06
+
+
+def _end_terms(buf, across, out_dim, in_dim):
+    return jnp.concatenate(
+        lax.all_to_all(
+            jnp.stack(jnp.split(buf, lax.axis_size(across), axis=out_dim)), across, 0, 0
+        ),
+        in_dim,
+    )
+
+
+weights_try_all = functools.partial(_end_terms, across="dp", out_dim=1, in_dim=0)
 
 
 def visible(blocks, seq_len):
@@ -62,13 +75,9 @@
         hidden * lax.rsqrt(square[:, None] / D + epsilon) * norm_gain.astype(jnp.float32)[None, :]
     ).astype(jnp.bfloat16)
     full_rows = lax.all_gather(normed, "mp", axis=1, tiled=True)
-    block_rows = lax.all_to_all(
-        full_rows.reshape(seq_len, data_count, row_width),
-        "dp",
-        split_axis=1,
-        concat_axis=0,
-        tiled=True,
-    ).reshape(data_count * seq_len, row_width)
+    block_rows = weights_try_all(full_rows.reshape(seq_len, data_count, row_width)).reshape(
+        data_count * seq_len, row_width
+    )
     language = languages[:, 0]
     alive = (jnp.arange(seq_len)[None, :] < lengths[:, None]).astype(jnp.bfloat16)
     alive_flat = alive.reshape(-1)

time: 481 us -> 498 us (1.035)
  local copies, waits for them, and re-layouts: 39.5 us -> 74.9 us
  waiting for transfers between devices: 234 us -> 216 us
    unnamed x24 -> x57, local copies, waits for them, and re-layouts: 7.59 us -> 42.3 us
    all_gather x1, waiting for transfers between devices: 70.8 us -> 39.3 us  [shards(): piece = lax.all_gather(normed, 'dp', axis=0, tiled=True)]
    all_to_all x1, waiting for transfers between devices: 92.5 us -> 105 us  [_end_terms(): lax.all_to_all(jnp.stack(jnp.split(buf, lax.axis_size(across), axis=out_d...]
  transfers between devices with their start and end apart: 4 -> 4, of which waited for: 4 -> 4; matrix products, arithmetic and copies ran while one was open for 2% -> 9% of each run, Pallas kernels for 0% -> 0%
where the time goes in v1:
time: 498 us; the launch traced here: 494 us
  waiting for transfers between devices  216 us (43%)
  matrix products  91 us (18%)
  local copies, waits for them, and re-layouts  74.9 us (15%)
  loops' own time  65.3 us (13%)
  blocking collectives  15 us (3%)
  between operations  13.9 us (3%)
  starting transfers between devices  9.82 us (2%)
  other arithmetic  8.44 us (2%)
    all_to_all x1, waiting for transfers between devices, _end_terms(): lax.all_to_all(jnp.stack(jnp.split(buf, lax.axis_size(across), axis=out_d...  105 us
    another operation x1, loops' own time, shards(): lax.fori_loop(0, turn_count, one_sequence, start_state)  65.3 us
    dot_general x32, matrix products, one_sequence(): lax.dot_general(left_rows, piece_part, (((0,), (0,)), ((), ())), preferre...  44 us
    unnamed x57, local copies, waits for them, and re-layouts  42.3 us
    unnamed x4, waiting for transfers between devices  40 us
    all_gather x1, waiting for transfers between devices, shards(): piece = lax.all_gather(normed, 'dp', axis=0, tiled=True)  39.3 us
    dot_general x32, matrix products, one_sequence(): jnp.dot(live_part, piece_part, preferred_element_type=jnp.float32)  38.8 us
    all_gather x1, waiting for transfers between devices, shards(): full_rows = lax.all_gather(normed, 'mp', axis=1, tiled=True)  31 us
  transfers between devices with their start and end apart: 4, of which 4 were waited for; matrix products, arithmetic and copies ran while one was open for 9% of the time, Pallas kernels for 0%

profile of v1, /device:TPU:1, one launch (start us, length us, event | category | flops | bytes accessed | tf_op | source)
XLA Modules:
  0.0 494.0 jit_solution(6878994738741618268)
XLA Ops:
  13.4 4.5 fusion.7
  17.9 3.6 copy.101
  22.8 39.3 %reduce-scatter.4.cloned.1.call-done = bf16[576,384]{1,0:T(8,128)(2,1)} async-done(((bf16[4608,384]{1,0:T(8,128)(2,1)}), bf16[576,384]{1,0:T(8,128)(2,1)}) %reduce-scatter.4.cloned.1.call-update) | async-done | bytes 442384
  62.1 1.3 copy.102
  63.7 15.0 %psum.7 = f32[384]{0:T(512)S(1)} all-reduce(f32[384]{0:T(512)S(1)} %multiply_reduce_fusion), channel_id=1, replica_groups=mesh['dp'=32,'mp'=8] {'mp'}, use_global_device_ids=true, to_apply=%region_4.5 | all-reduce | flops 384 | bytes 3072 | tf_op jit(solution)/shard_map/psum | solution.py:73
  80.6 31.0 %all-gather.3.cloned.1.call-done = bf16[384,4608]{0,1:T(8,128)(2,1)} async-done(((bf16[384,576]{0,1:T(8,128)(2,1)}), bf16[384,4608]{0,1:T(8,128)(2,1)}) %all-gather.3.cloned.1.call-update) | async-done | bytes 3538960 | tf_op jit(solution)/shard_map/all_gather | solution.py:77
  111.6 1.7 fusion.43
  113.3 1.5 fusion.42
  114.9 1.5 fusion.41
  116.4 1.5 fusion.40
  118.0 1.5 fusion.39
  119.5 1.5 fusion.38
  121.0 1.5 fusion.37
  122.6 1.6 fusion.36
  124.1 1.6 fusion.35
  125.7 1.6 fusion.34
  127.3 1.6 fusion.33
  128.8 1.5 fusion.32
  130.4 1.6 fusion.31
  131.9 1.5 fusion.30
  133.5 1.6 fusion.29
  135.0 1.5 fusion.28
  147.1 9.7 %all-to-all-start = ((bf16[32,384,1,144]{1,3,2,0:T(8,128)(2,1)}), bf16[32,384,1,144]{1,3,2,0:T(8,128)(2,1)S(1)}, u32[]{:S(2)}, u32[]{:S(2)}) async-start(bf16[32,384,1,144]{1,3,2,0:T(8,128)(2,1)} %fusion.12), calls=%async_computation | async-start | bytes 7077888 | tf_op jit(solution)/shard_map/all_to_all | solution.py:20
  157.5 1.3 fusion.44
  158.8 1.4 reshape.142
  160.2 1.5 broadcast_multiply_fusion.1
  161.7 105.2 %all-to-all-done = bf16[32,384,1,144]{1,3,2,0:T(8,128)(2,1)S(1)} async-done(((bf16[32,384,1,144]{1,3,2,0:T(8,128)(2,1)}), bf16[32,384,1,144]{1,3,2,0:T(8,128)(2,1)S(1)}, u32[]{:S(2)}, u32[]{:S(2)}) %all-to-all-start) | async-done | bytes 3538976 | tf_op jit(solution)/shard_map/all_to_all | solution.py:20
  267.9 1.6 broadcast_divide_fusion
  269.5 2.0 broadcast_multiply_fusion
  271.5 39.3 %all-gather.5.cloned.1.call-done = bf16[12288,576]{1,0:T(8,128)(2,1)} async-done(((bf16[384,576]{1,0:T(8,128)(2,1)}), bf16[12288,576]{1,0:T(8,128)(2,1)}) %all-gather.5.cloned.1.call-update) | async-done | bytes 14155792 | tf_op jit(solution)/shard_map/all_gather | solution.py:95
  311.0 174.4 %while.17 = (s32[]{:T(128)}, f32[8,144,576]{2,1,0:T(8,128)S(1)}, f32[8,576]{1,0:T(8,128)S(1)}, s32[32]{0:T(128)S(1)}, bf16[12288,144]{0,1:T(8,128)(2,1)}, /*inde...) while((s32[]{:T(128)}, f32[8,144,576]{2,1,0:T(8,128)S(1)}, ...), condition=%wide.region_6.7_spmd, body=%wide.region_5.6_spmd.sunk | while | flops 64226900 | bytes 2523245 | solution.py:119
  313.6 1.4 fusion.63
  319.1 1.4 fusion.63
  324.5 1.4 fusion.63
  330.0 1.4 fusion.63
  335.4 1.4 fusion.63
  340.9 1.4 fusion.63
  346.3 1.4 fusion.63
  351.8 1.4 fusion.63
  357.2 1.4 fusion.63
  362.7 1.4 fusion.63
  368.1 1.4 fusion.63
  373.6 1.4 fusion.63
  379.0 1.4 fusion.63
  384.5 1.4 fusion.63
  389.9 1.4 fusion.63
  395.4 1.4 fusion.63
  400.8 1.4 fusion.63
  406.3 1.4 fusion.63
  411.7 1.4 fusion.63
  417.2 1.4 fusion.63
  422.6 1.4 fusion.63
  428.1 1.4 fusion.63
  433.5 1.4 fusion.63
  438.9 1.4 fusion.63
  444.4 1.4 fusion.63
  449.8 1.4 fusion.63
  455.3 1.4 fusion.63
  460.7 1.4 fusion.63
  466.2 1.4 fusion.63
  471.6 1.4 fusion.63
  477.1 1.4 fusion.63
  482.5 1.4 fusion.63
  485.4 2.1 subtract_divide_fusion
  (353 shorter events, 86.9 us)
Async XLA Ops:
  7.2 55.0 %reduce-scatter.4.cloned.1.call-start = ((), (), s32[]{:S(2)}) async-start(), calls=%async_computation.4 | async-start | bytes 3981312
  21.5 1.0 copy-start.3
  21.5 1.3 copy-start.5
  21.6 90.1 %all-gather.3.cloned.1.call-start = ((), (), s32[]{:S(2)}) async-start(), calls=%async_computation.2 | async-start | bytes 3981312 | tf_op jit(solution)/shard_map/all_gather | solution.py:77
  78.9 1.0 copy-start
  79.9 230.9 %all-gather.5.cloned.1.call-start = ((), (), s32[]{:S(2)}) async-start(), calls=%async_computation.3 | async-start | bytes 16220160 | tf_op jit(solution)/shard_map/all_gather | solution.py:95
  111.6 25.0 %copy-start.1 = (bf16[384,4608]{0,1:T(8,128)(2,1)S(1)}, bf16[384,4608]{0,1:T(8,128)(2,1)}, u32[]{:S(2)}) copy-start(bf16[384,4608]{0,1:T(8,128)(2,1)} %all-gather.3.cloned.1.call-done) | copy-start | bytes 10616836
  147.1 9.7 %copy-start.6 = (s32[32]{0:T(128)S(1)}, s32[32]{0:T(128)}, u32[]{:S(2)}) copy-start(s32[32]{0:T(128)} %param.18) | copy-start | bytes 388
  147.1 9.7 %copy-start.7 = (s32[32,1]{0,1:T(1,128)S(1)}, s32[32,1]{0,1:T(1,128)}, u32[]{:S(2)}) copy-start(s32[32,1]{0,1:T(1,128)} %param.17) | copy-start | bytes 388
  147.1 119.9 %all-to-all-start = ((bf16[32,384,1,144]{1,3,2,0:T(8,128)(2,1)}), bf16[32,384,1,144]{1,3,2,0:T(8,128)(2,1)S(1)}, u32[]{:S(2)}, u32[]{:S(2)}) async-start(bf16[32,384,1,144]{1,3,2,0:T(8,128)(2,1)} %fusion.12), calls=%async_computation | async-start | bytes 7077888 | tf_op jit(solution)/shard_map/all_to_all | solution.py:20
  156.9 0.5 copy-start.9
  266.9 0.9 copy-start.2
  267.5 2.0 copy-start.4
  269.5 41.5 %copy-start.8 = (s32[32,1]{0,1:T(1,128)S(1)}, s32[32,1]{0,1:T(1,128)}, u32[]{:S(2)}) copy-start(s32[32,1]{0,1:T(1,128)} %param.17) | copy-start | bytes 388
Sparse Core Ops, SparseCore 0:
  21.7 40.4 reduce-scatter.3
  80.0 31.5 all-gather.2
  114.8 195.9 all-gather.4
